TPU v7x, 128 devices: a whole 4x4x4 slice. The times are simulated.
128 devices in a mesh: dom: 64 (over z, x, y), rep: 2 (over core).
Axes of the slice: x: 4, y: 4, z: 4, core: 2. Of those that a mesh axis runs over, the one named last changes fastest.
Arguments:
- embeds: bfloat16 [65536, 1024], P(('dom', 'rep')), may hold values from -6 to 6
- weight_in: bfloat16 [1024, 4096], replicated, may hold values from -0.1875 to 0.1875
- weight_out: bfloat16 [4096, 512], replicated, may hold values from -0.09375 to 0.09375
- prototypes: bfloat16 [1000, 512], replicated, may hold values from -4 to 4
- tile_column: int32 [512, 8], P(('dom', 'rep')), may hold values from 0 to 11, as said below
- tile_weight: bfloat16 [512, 8, 128, 128], P(('dom', 'rep')), may hold values from 0 to 1
- send_rows: int32 [128, 128, 8], P(('dom', 'rep')), may hold values from 0 to 511
- send_count: int32 [128, 128], P(('dom', 'rep')), may hold values from 1 to 8, as said below
- label_rows: int32 [8192], P(('dom', 'rep')), may hold values from 0 to 511, as said below
- label_class: int32 [8192], P(('dom', 'rep')), may hold values from 0 to 999
Outputs:
- embed_grad: bfloat16 [65536, 1024], P(('dom', 'rep'))
- grad_weight_out: float32 [4096, 512], P(('dom', 'rep'))
Inputs may be any that keep to these rules, and one draw needn't show every extreme that they name: `tile_column`: in each row block b the first tile names block b mod 4, tiles 1 to 3 name blocks below 4, the others name received blocks; every received block is named by some tile of its partition. `send_count`: every partition fills all 8 slots for at least one other partition. `label_rows`: distinct within a partition.
All inputs are finite; a program needn't handle non-finite values.
Results may differ from a plain program's by a relative error of at most 0.006.
The roundings to bfloat16 on the way count: a program that leaves them out, or rounds other values in their place, can miss the bound.
Values may be sent and summed in bfloat16 or wider, within the bound.
A program may use at most 128 MiB of HBM per device.

v0:
```python
import math

import jax
import jax.numpy as jnp
from jax import lax
from jax.sharding import PartitionSpec as P

gelu_inner = 0.7978845608028654
gelu_cubic = 0.044715


def gelu_value(values):
    inner_arg = gelu_inner * (values + gelu_cubic * values * values * values)
    return 0.5 * values * (1.0 + jnp.tanh(inner_arg))


def gelu_slope(values):
    inner_arg = gelu_inner * (values + gelu_cubic * values * values * values)
    tangent = jnp.tanh(inner_arg)
    return 0.5 * (1.0 + tangent) + 0.5 * values * (1.0 - tangent * tangent) * gelu_inner * (
        1.0 + 3.0 * gelu_cubic * values * values
    )


def body(
    embeds,
    weight_in,
    weight_out,
    prototypes,
    tile_column,
    tile_weight,
    send_rows,
    send_count,
    label_rows,
    label_class,
):
    node_count = embeds.shape[0]
    block_count = tile_weight.shape[0]
    tile_count = tile_weight.shape[1]
    block_size = tile_weight.shape[2]
    width_out = weight_out.shape[1]
    dom_count = lax.axis_size("dom")
    rep_count = lax.axis_size("rep")
    peer_count = dom_count * rep_count
    slot_count = send_rows.shape[2]
    pre_act = jnp.dot(embeds, weight_in, preferred_element_type=jnp.float32)
    hidden = gelu_value(pre_act).astype(jnp.bfloat16)
    projected = jnp.dot(hidden, weight_out, preferred_element_type=jnp.float32)
    rowsum = jnp.sum(tile_weight, axis=(1, 3), dtype=jnp.float32).reshape(node_count)
    scaling = lax.rsqrt(1.0 + rowsum)
    unit_rows = (projected * scaling[:, None]).astype(jnp.bfloat16)
    slot_mask = (
        lax.broadcasted_iota(jnp.int32, (peer_count, slot_count), 1) < send_count[0][:, None]
    )
    flat_sends = send_rows[0].reshape(peer_count * slot_count)
    outgoing = jnp.take(unit_rows, flat_sends, axis=0).reshape(peer_count, slot_count, width_out)
    outgoing = jnp.where(slot_mask[:, :, None], outgoing, jnp.zeros_like(outgoing))
    incoming = lax.all_to_all(outgoing, ("dom", "rep"), split_axis=0, concat_axis=0, tiled=True)
    incoming = incoming.reshape(peer_count * slot_count, width_out)
    extended = jnp.concatenate([unit_rows, incoming], axis=0).reshape(-1, block_size, width_out)
    total_blocks = extended.shape[0]
    flat_columns = tile_column.reshape(block_count * tile_count)
    sources = jnp.take(extended, flat_columns, axis=0).reshape(
        block_count, tile_count, block_size, width_out
    )
    neighbour = jnp.einsum(
        "rtab,rtbd->rad", tile_weight, sources, preferred_element_type=jnp.float32
    )
    row_term = rowsum[:, None] * unit_rows.astype(jnp.float32) - neighbour.reshape(
        node_count, width_out
    )
    unit_blocks = unit_rows.reshape(block_count, block_size, width_out)
    column_sum = jnp.sum(tile_weight, axis=2, dtype=jnp.float32)
    column_term = column_sum[:, :, :, None] * sources.astype(jnp.float32) - jnp.einsum(
        "rtab,rad->rtbd", tile_weight, unit_blocks, preferred_element_type=jnp.float32
    )
    selector = (
        flat_columns[:, None]
        == lax.broadcasted_iota(jnp.int32, (block_count * tile_count, total_blocks), 1)
    ).astype(jnp.float32)
    gathered_terms = jnp.einsum(
        "tc,tf->cf",
        selector,
        column_term.reshape(block_count * tile_count, block_size * width_out),
        precision=lax.Precision.HIGHEST,
    )
    own_term = gathered_terms[:block_count].reshape(node_count, width_out)
    returned = (
        gathered_terms[block_count:].reshape(peer_count, slot_count, width_out).astype(jnp.bfloat16)
    )
    arrived = lax.all_to_all(returned, ("dom", "rep"), split_axis=0, concat_axis=0, tiled=True)
    back_rows = arrived.reshape(peer_count * slot_count, width_out)
    placement = (
        flat_sends[None, :]
        == lax.broadcasted_iota(jnp.int32, (node_count, peer_count * slot_count), 0)
    ) & slot_mask.reshape(peer_count * slot_count)[None, :]
    back_sum = jnp.dot(
        placement.astype(jnp.bfloat16), back_rows, preferred_element_type=jnp.float32
    )
    grad_proj = (row_term + own_term + back_sum) * scaling[:, None]
    class_table = (
        label_class[:, None]
        == lax.broadcasted_iota(jnp.int32, (label_class.shape[0], prototypes.shape[0]), 1)
    ).astype(jnp.bfloat16)
    targets = jnp.dot(class_table, prototypes, preferred_element_type=jnp.float32)
    grad_proj = grad_proj.at[label_rows].add(jnp.take(projected, label_rows, axis=0) - targets)
    grad_node = grad_proj.astype(jnp.bfloat16)
    grad_hidden = lax.dot_general(
        grad_node, weight_out, (((1,), (1,)), ((), ())), preferred_element_type=jnp.float32
    )
    grad_pre = (grad_hidden * gelu_slope(pre_act)).astype(jnp.bfloat16)
    embed_grad = lax.dot_general(
        grad_pre, weight_in, (((1,), (1,)), ((), ())), preferred_element_type=jnp.float32
    ).astype(jnp.bfloat16)
    factor = 1.0 / math.sqrt(node_count * peer_count)
    grad_weight = lax.psum_scatter(
        lax.dot_general(
            hidden, grad_node, (((0,), (0,)), ((), ())), preferred_element_type=jnp.float32
        ),
        ("dom", "rep"),
        scatter_dimension=0,
        tiled=True,
    )
    return (embed_grad, grad_weight * factor)


def solution(mesh):
    placed = (
        P(("dom", "rep"), None),
        P(),
        P(),
        P(),
        P(("dom", "rep"), None),
        P(("dom", "rep"), None, None, None),
        P(("dom", "rep"), None, None),
        P(("dom", "rep"), None),
        P(("dom", "rep")),
        P(("dom", "rep")),
    )
    return jax.shard_map(
        body,
        mesh=mesh,
        in_specs=placed,
        out_specs=(P(("dom", "rep"), None), P(("dom", "rep"), None)),
        check_vma=False,
    )
```

profile of v0, /device:TPU:0, one launch (start us, length us, event | category | flops | bytes accessed | tf_op | source)
XLA Modules:
  0.0 788.0 jit_solution(5872668848528346889)
XLA Ops:
  7.2 0.0 copy-start
  7.2 0.8 compare_and_fusion
  8.0 0.8 copy.16
  8.8 0.1 copy.15
  8.9 0.7 iota_compare_fusion.3
  9.6 1.5 convert_reduce_fusion.1
  11.2 0.1 reshape_squeeze.8
  11.3 0.0 copy-start.7
  11.3 7.0 fusion.40
  18.4 2.7 multiply_convert_fusion.1
  21.1 0.5 copy-done.9
  21.6 4.0 gather_fusion
  25.6 1.2 fusion.22
  26.8 11.1 %all-to-all-start = ((bf16[128,8,512]{2,1,0:T(8,128)(2,1)}), bf16[128,8,512]{2,1,0:T(8,128)(2,1)S(1)}, u32[]{:S(2)}, u32[]{:S(2)}) async-start(bf16[128,8,512]{2,1,0:T(8,128)(2,1)} %fusion.22), calls=%async_computation | async-start | bytes 2097152 | tf_op jit(solution)/shard_map/all_to_all | solution.py:58
  38.0 0.1 reshape.167
  38.1 0.1 reshape.165
  38.1 0.1 lt.86
  38.2 0.1 reshape_squeeze.9
  38.3 0.0 copy-done.8
  38.4 0.7 gather_fusion.2
  39.1 18.0 %all-to-all-done = bf16[128,8,512]{2,1,0:T(8,128)(2,1)S(1)} async-done(((bf16[128,8,512]{2,1,0:T(8,128)(2,1)}), bf16[128,8,512]{2,1,0:T(8,128)(2,1)S(1)}, u32[]{:S(2)}, u32[]{:S(2)}) %all-to-all-start) | async-done | bytes 1048608 | tf_op jit(solution)/shard_map/all_to_all | solution.py:58
  57.1 1.0 copy-done.4
  58.0 1.3 pad_maximum_fusion
  59.4 2.8 gather_fusion.1
  62.1 6.5 copy.17
  68.6 7.0 bitcast_subtract_fusion
  75.7 10.3 %copy.27 = f32[4,8,128,512]{3,1,2,0:T(8,128)} copy(f32[4,8,128,512]{2,3,1,0:T(8,128)} %bitcast_subtract_fusion) | data formatting | bytes 16777216
  86.0 5.5 fusion.30
  91.5 0.0 copy-start.2
  91.5 2.0 copy-done.2
  93.4 0.2 slice.18
  93.6 1.5 convert_element_type.37
  95.1 5.9 all-to-all-start.1
  101.0 0.0 reduce-scatter.2.cloned.1.call-start
  101.1 1.6 convolution_subtract_fusion
  102.6 2.7 slice.15
  105.3 1.9 reshape.170
  107.3 3.7 fusion.7
  111.0 0.2 fusion.20
  111.2 8.4 %all-to-all-done.1 = bf16[128,8,512]{2,1,0:T(8,128)(2,1)} async-done(((bf16[128,8,512]{2,1,0:T(8,128)(2,1)}), bf16[128,8,512]{2,1,0:T(8,128)(2,1)}, u32[]{:S(2)}, u32[]{:S(2)}) %all-to-all-start.1) | async-done | bytes 1048608 | tf_op jit(solution)/shard_map/all_to_all | solution.py:91
  119.7 1.9 fusion.17
  121.6 1.4 scatter_fusion
  123.0 10.3 %fusion.25 = f32[4096,512]{1,0:T(8,128)} fusion(f32[512,512]{1,0:T(8,128)S(1)} %scatter_fusion, f32[512,4096]{1,0:T(8,128)} %copy-done.9), kind=kOutput, calls=%fused_computation.38 | convolution fusion | flops 2166620160 | bytes 17825792 | tf_op jit(solution)/shard_map/dot_general | solution.py:117
  133.3 0.0 reduce-scatter.2.cloned.1.call-update
  133.3 0.0 copy-start.1
  133.4 17.4 %fusion.13 = bf16[512,1024]{1,0:T(8,128)(2,1)} fusion(bf16[1024,4096]{1,0:T(8,128)(2,1)} %param.11, f32[512,4096]{1,0:T(8,128)} %copy-done.9, bf16[4096,512]{1,0:T(8,128)(2,1)} %param.12, f32[512,512]{1,0:T(8,128)S(1)} %scatter_fusion), kind=kOutput, calls=%fused_computation.26 | convolution fusion | flops 6483083264 | bytes 23068672 | tf_op jit(solution)/shard_map/dot_general | solution.py:112
  150.7 629.0 %reduce-scatter.2.cloned.1.call-done = f32[32,512]{1,0:T(8,128)} async-done(((f32[4096,512]{1,0:T(8,128)}), f32[32,512]{1,0:T(8,128)}) %reduce-scatter.2.cloned.1.call-update) | async-done | bytes 65552 | tf_op jit(solution)/shard_map/reduce_scatter | solution.py:116
  779.7 1.5 broadcast_multiply_fusion
  (21 shorter events, 0.1 us)
Async XLA Ops:
  7.2 4.1 copy-start
  11.3 7.1 copy-start.7
  18.4 3.2 copy-start.9
  21.6 16.4 %copy-start.5 = (s32[4,8]{1,0:T(4,128)S(1)}, s32[4,8]{1,0:T(4,128)}, u32[]{:S(2)}) copy-start(s32[4,8]{1,0:T(4,128)} %param.14) | copy-start | bytes 388
  21.6 16.7 %copy-start.8 = (s32[64]{0:T(128)S(1)}, s32[64]{0:T(128)}, u32[]{:S(2)}) copy-start(s32[64]{0:T(128)} %param.18) | copy-start | bytes 772
  26.8 30.2 %all-to-all-start = ((bf16[128,8,512]{2,1,0:T(8,128)(2,1)}), bf16[128,8,512]{2,1,0:T(8,128)(2,1)S(1)}, u32[]{:S(2)}, u32[]{:S(2)}) async-start(bf16[128,8,512]{2,1,0:T(8,128)(2,1)} %fusion.22), calls=%async_computation | async-start | bytes 2097152 | tf_op jit(solution)/shard_map/all_to_all | solution.py:58
  57.1 1.0 copy-start.4
  62.1 6.5 copy-start.3
  86.0 15.1 %copy-start.6 = (s32[64]{0:T(128)S(1)}, s32[64]{0:T(128)}, u32[]{:S(2)}) copy-start(s32[64]{0:T(128)} %param.19) | copy-start | bytes 772
  91.5 2.0 copy-start.2
  95.1 24.6 %all-to-all-start.1 = ((bf16[128,8,512]{2,1,0:T(8,128)(2,1)}), bf16[128,8,512]{2,1,0:T(8,128)(2,1)}, u32[]{:S(2)}, u32[]{:S(2)}) async-start(bf16[128,8,512]{2,1,0:T(8,128)(2,1)} %convert_element_type.37), calls=%async_computation.1 | async-start | bytes 2097152 | tf_op jit(solution)/shard_map/all_to_all | solution.py:91
  101.0 678.7 %reduce-scatter.2.cloned.1.call-start = ((), (), s32[]{:S(2)}) async-start(), calls=%async_computation.3 | async-start | bytes 8454144 | tf_op jit(solution)/shard_map/reduce_scatter | solution.py:116
  133.3 647.8 %copy-start.1 = (bf16[512,1024]{1,0:T(8,128)(2,1)S(1)}, bf16[512,1024]{1,0:T(8,128)(2,1)}, u32[]{:S(2)}) copy-start(bf16[512,1024]{1,0:T(8,128)(2,1)} %param.10) | copy-start | bytes 3145732
Sparse Core Ops, SparseCore 0:
  133.5 646.1 reduce-scatter.1
where the time goes:
time: 789 us; the launch traced here: 788 us
  waiting for transfers between devices  655 us (83%)
  matrix products  57.2 us (7%)
  local copies, waits for them, and re-layouts  35.3 us (4%)
  starting transfers between devices  17.1 us (2%)
  between operations  14.3 us (2%)
  other arithmetic  8.75 us (1%)
    reduce_scatter x1, waiting for transfers between devices, body(): lax.psum_scatter(lax.dot_general(hidden, grad_node, (((0,), (0,)), ((), (...  629 us
    all_to_all x1, waiting for transfers between devices, body(): lax.all_to_all(outgoing, ('dom', 'rep'), split_axis=0, concat_axis=0, til...  18 us
    dot_general x1, matrix products, body(): lax.dot_general(grad_pre, weight_in, (((1,), (1,)), ((), ())), preferred_...  17.4 us
  transfers between devices with their start and end apart: 3, of which 3 were waited for; matrix products, arithmetic and copies ran while one was open for 4% of the time, Pallas kernels for 0%

commit v1 on v0

--- a/solution.py
+++ b/solution.py
@@ -1,8 +1,11 @@
+import functools
 import math
 
 import jax
 import jax.numpy as jnp
 from jax import lax
+from jax.experimental import pallas as pl
+from jax.experimental.pallas import tpu as pltpu
 from jax.sharding import PartitionSpec as P
 
 gelu_inner = 0.7978845608028654
@@ -20,6 +23,148 @@
     return 0.5 * (1.0 + tangent) + 0.5 * values * (1.0 - tangent * tangent) * gelu_inner * (
         1.0 + 3.0 * gelu_cubic * values * values
     )
+
+
+MESH = pl.DeviceIdType.MESH
+COLOURS = (
+    ((0, 1, 2), slice(0, 16), slice(0, 384)),
+    ((1, 2, 0), slice(16, 32), slice(0, 384)),
+    ((2, 0, 1), slice(0, 32), slice(384, 512)),
+)
+STRIDES = (16, 4, 1)
+
+
+def place():
+    dom = lax.axis_index("dom")
+    return (dom // 16, lax.rem(dom // 4, 4), lax.rem(dom, 4)), lax.axis_index("rep")
+
+
+def moved(coords, axis, step):
+    there = [lax.rem(c + step, 4) if a == axis else c for a, c in enumerate(coords)]
+    return there[0] * 16 + there[1] * 4 + there[2]
+
+
+def enter(coords, core):
+    barrier = pltpu.get_barrier_semaphore()
+    here = coords[0] * 16 + coords[1] * 4 + coords[2]
+    pl.semaphore_signal(barrier, inc=1, device_id=(here, 1 - core), device_id_type=MESH)
+    for axis in range(3):
+        for step in (1, 2, 3):
+            pl.semaphore_signal(
+                barrier, inc=1, device_id=(moved(coords, axis, step), core), device_id_type=MESH
+            )
+    return barrier
+
+
+def scatter_sum_kernel(
+    factor, part_ref, out_ref, mate, b0, b1, b2, r10, r11, r12, s10, s11, s12,
+    r20, r21, r22, s20, s21, s22, r30, r31, r32, mate_send, mate_recv, send_sem, recv_sem
+):
+    coords, core = place()
+    here = coords[0] * 16 + coords[1] * 4 + coords[2]
+    barrier = enter(coords, core)
+    pl.semaphore_wait(barrier, 10)
+    swap = pltpu.make_async_remote_copy(
+        src_ref=part_ref.at[:, 1 - core],
+        dst_ref=mate,
+        send_sem=mate_send,
+        recv_sem=mate_recv,
+        device_id=(here, 1 - core),
+        device_id_type=MESH,
+    )
+    swap.start()
+    swap.wait()
+    first = (b0, b1, b2)
+
+    def join(chip, carry):
+        z, x, y = chip // 16, lax.rem(chip // 4, 4), lax.rem(chip, 4)
+        at = (z, x, y)
+        total = (
+            part_ref[chip, core].astype(jnp.float32) + mate[chip].astype(jnp.float32)
+        ).astype(jnp.bfloat16)
+        for buffer, (order, rows, cols) in zip(first, COLOURS):
+            spot = at[order[0]] * 16 + at[order[1]] * 4 + at[order[2]]
+            buffer[spot] = total[rows, cols]
+        return carry
+
+    lax.fori_loop(0, 64, join, 0)
+    held = [first, (s10, s11, s12), (s20, s21, s22)]
+    landing = [(r10, r11, r12), (r20, r21, r22), (r30, r31, r32)]
+
+    def launch(stage, colour):
+        axis = COLOURS[colour][0][stage]
+        size = STRIDES[stage]
+        copies = []
+        for step in (1, 2, 3):
+            peer = lax.rem(coords[axis] + step, 4)
+            copies.append(
+                pltpu.make_async_remote_copy(
+                    src_ref=held[stage][colour].at[pl.ds(peer * size, size)],
+                    dst_ref=landing[stage][colour].at[step - 1],
+                    send_sem=send_sem.at[stage, colour, step - 1],
+                    recv_sem=recv_sem.at[stage, colour, step - 1],
+                    device_id=(moved(coords, axis, step), core),
+                    device_id_type=MESH,
+                )
+            )
+        for copy in copies:
+            copy.start()
+        return copies
+
+    def add(stage, colour, spot):
+        axis = COLOURS[colour][0][stage]
+        mine = coords[axis] * STRIDES[stage] + spot
+        total = held[stage][colour][mine].astype(jnp.float32)
+        for step in range(3):
+            total = total + landing[stage][colour][step, spot].astype(jnp.float32)
+        return total
+
+    flying = [launch(0, colour) for colour in range(3)]
+    for stage in range(3):
+        after = []
+        for colour in range(3):
+            for copy in flying[colour]:
+                copy.wait()
+            if stage < 2:
+
+                def fold(spot, carry, stage=stage, colour=colour):
+                    held[stage + 1][colour][spot] = add(stage, colour, spot).astype(jnp.bfloat16)
+                    return carry
+
+                lax.fori_loop(0, STRIDES[stage], fold, 0)
+                after.append(launch(stage + 1, colour))
+            else:
+                _, rows, cols = COLOURS[colour]
+                out_ref[rows, cols] = add(stage, colour, 0) * factor
+        flying = after
+
+
+def scatter_sum(partial, factor):
+    shapes = [(c[1].stop - c[1].start, c[2].stop - c[2].start) for c in COLOURS]
+    vmem = lambda *lead: [pltpu.VMEM(lead + s, jnp.bfloat16) for s in shapes]
+    return pl.pallas_call(
+        functools.partial(scatter_sum_kernel, factor),
+        out_shape=jax.ShapeDtypeStruct((32, 512), jnp.float32),
+        in_specs=[pl.BlockSpec(memory_space=pltpu.VMEM)],
+        out_specs=pl.BlockSpec(memory_space=pltpu.VMEM),
+        scratch_shapes=[pltpu.VMEM((64, 32, 512), jnp.bfloat16)]
+        + vmem(64)
+        + vmem(3, 16)
+        + vmem(16)
+        + vmem(3, 4)
+        + vmem(4)
+        + vmem(3, 1)
+        + [
+            pltpu.SemaphoreType.DMA,
+            pltpu.SemaphoreType.DMA,
+            pltpu.SemaphoreType.DMA((3, 3, 3)),
+            pltpu.SemaphoreType.DMA((3, 3, 3)),
+        ],
+        compiler_params=pltpu.CompilerParams(
+            collective_id=0, has_side_effects=True, vmem_limit_bytes=48 << 20
+        ),
+        name="scatter_sum",
+    )(partial)
 
 
 def body(
@@ -113,15 +258,11 @@
         grad_pre, weight_in, (((1,), (1,)), ((), ())), preferred_element_type=jnp.float32
     ).astype(jnp.bfloat16)
     factor = 1.0 / math.sqrt(node_count * peer_count)
-    grad_weight = lax.psum_scatter(
-        lax.dot_general(
-            hidden, grad_node, (((0,), (0,)), ((), ())), preferred_element_type=jnp.float32
-        ),
-        ("dom", "rep"),
-        scatter_dimension=0,
-        tiled=True,
-    )
-    return (embed_grad, grad_weight * factor)
+    partial = lax.dot_general(
+        hidden, grad_node, (((0,), (0,)), ((), ())), preferred_element_type=jnp.float32
+    ).astype(jnp.bfloat16)
+    grad_weight = scatter_sum(partial.reshape(peer_count // 2, 2, -1, width_out), factor)
+    return (embed_grad, grad_weight)
 
 
 def solution(mesh):

time: 789 us -> 170 us (0.22)
  waiting for transfers between devices: 655 us -> 26.4 us
  Pallas kernels: 0 us -> 27.4 us
  between operations: 14.3 us -> 0.89 us
    reduce_scatter x1 -> x0, waiting for transfers between devices: 629 us -> none  [body(): lax.psum_scatter(lax.dot_general(hidden, grad_node, (((0,), (0,)), ((), (...]
    pallas_call x0 -> x1, Pallas kernels: none -> 27.4 us  [scatter_sum(): pl.pallas_call(functools.partial(scatter_sum_kernel, factor), out_shape=j...]
  transfers between devices with their start and end apart: 3 -> 2, of which waited for: 3 -> 2; matrix products, arithmetic and copies ran while one was open for 4% -> 7% of each run, Pallas kernels for 0% -> 0%
where the time goes in v1:
time: 170 us; the launch traced here: 169 us
  matrix products  54.1 us (32%)
  local copies, waits for them, and re-layouts  35.9 us (21%)
  Pallas kernels  27.4 us (16%)
  waiting for transfers between devices  26.4 us (16%)
  starting transfers between devices  17.1 us (10%)
  other arithmetic  7.27 us (4%)
    pallas_call x1, Pallas kernels, scatter_sum(): pl.pallas_call(functools.partial(scatter_sum_kernel, factor), out_shape=j...  27.4 us
    all_to_all x1, waiting for transfers between devices, body(): lax.all_to_all(outgoing, ('dom', 'rep'), split_axis=0, concat_axis=0, til...  18 us
    dot_general x1, matrix products, body(): lax.dot_general(grad_pre, weight_in, (((1,), (1,)), ((), ())), preferred_...  17.2 us
    unnamed x23, local copies, waits for them, and re-layouts  15.2 us
    all_to_all x1, starting transfers between devices, body(): lax.all_to_all(outgoing, ('dom', 'rep'), split_axis=0, concat_axis=0, til...  11.1 us
    gather x2, local copies, waits for them, and re-layouts, body(): jnp.take(extended, flat_columns, axis=0)  9.25 us
    all_to_all x1, waiting for transfers between devices, body(): lax.all_to_all(returned, ('dom', 'rep'), split_axis=0, concat_axis=0, til...  8.48 us
    dot_general x1, matrix products, body(): lax.dot_general(hidden, grad_node, (((0,), (0,)), ((), ())), preferred_el...  7.36 us
  transfers between devices with their start and end apart: 2, of which 2 were waited for; matrix products, arithmetic and copies ran while one was open for 7% of the time, Pallas kernels for 0%

profile of v1, /device:TPU:0, one launch (start us, length us, event | category | flops | bytes accessed | tf_op | source)
XLA Modules:
  0.0 169.2 jit_solution(10818205611010982162)
XLA Ops:
  0.6 0.0 copy-start
  0.6 0.8 compare_and_fusion
  1.4 0.8 copy.16
  2.2 0.1 copy.15
  2.3 0.7 iota_compare_fusion.3
  3.1 1.5 convert_reduce_fusion.1
  4.6 0.1 reshape_squeeze.8
  4.8 0.0 copy-done
  4.8 0.0 copy-start.7
  4.8 7.0 %fusion.39 = f32[512,4096]{1,0:T(8,128)S(1)} fusion(bf16[512,1024]{1,0:T(8,128)(2,1)S(1)} %copy-done, bf16[1024,4096]{1,0:T(8,128)(2,1)} %param.11), kind=kOutput, calls=%fused_computation.67 | convolution fusion | flops 4294967296 | bytes 17825792 | tf_op jit(solution)/shard_map/dot_general | solution.py:191
  11.8 0.0 copy-done.7
  11.8 0.0 copy-start.9
  11.9 2.7 %multiply_convert_fusion.1 = (bf16[512,512]{1,0:T(8,128)(2,1)S(1)}, f32[512,512]{1,0:T(8,128)S(1)}) fusion(f32[512]{0:T(512)S(1)} %add_rsqrt_fusion, bf16[4096,512]{1,0:T(8,128)(2,1)S(1)} %copy-done.7, f32[512,4096]{1,0:T(8,128)S(1)} %fusion.39), kind=kOutput, calls=%fused_computation.37 | convolution fusion | flops 2166882304 | bytes 14157824 | tf_op jit(solution)/shard_map/dot_general | solution.py:193
  14.6 0.5 copy-done.9
  15.1 4.0 %gather_fusion = bf16[1024,512]{1,0:T(8,128)(2,1)S(1)} fusion(bf16[512,512]{1,0:T(8,128)(2,1)S(1)} %get-tuple-element.4, s32[1024]{0:T(1024)S(1)} %broadcast_clamp_fusion), kind=kCustom, calls=%fused_computation | custom fusion | bytes 2101248 | tf_op jit(solution)/shard_map/jit(_take)/gather | solution.py:201
  19.0 1.2 fusion.22
  20.3 11.1 %all-to-all-start = ((bf16[128,8,512]{2,1,0:T(8,128)(2,1)}), bf16[128,8,512]{2,1,0:T(8,128)(2,1)S(1)}, u32[]{:S(2)}, u32[]{:S(2)}) async-start(bf16[128,8,512]{2,1,0:T(8,128)(2,1)} %fusion.22), calls=%async_computation | async-start | bytes 2097152 | tf_op jit(solution)/shard_map/all_to_all | solution.py:203
  31.4 0.1 reshape.170
  31.5 0.1 reshape.168
  31.6 0.1 lt.86
  31.7 0.1 reshape_squeeze.9
  31.8 0.0 copy-done.8
  31.8 0.7 gather_fusion.2
  32.6 18.0 %all-to-all-done = bf16[128,8,512]{2,1,0:T(8,128)(2,1)S(1)} async-done(((bf16[128,8,512]{2,1,0:T(8,128)(2,1)}), bf16[128,8,512]{2,1,0:T(8,128)(2,1)S(1)}, u32[]{:S(2)}, u32[]{:S(2)}) %all-to-all-start) | async-done | bytes 1048608 | tf_op jit(solution)/shard_map/all_to_all | solution.py:203
  50.5 1.0 copy-done.4
  51.5 1.3 pad_maximum_fusion
  52.8 2.8 %gather_fusion.1 = bf16[32,128,512]{2,1,0:T(8,128)(2,1)} fusion(bf16[12,128,512]{2,1,0:T(8,128)(2,1)S(1)} %bitcast.55, s32[1024]{0:T(1024)S(1)} %pad_clamp_fusion.1), kind=kCustom, calls=%fused_computation.1 | custom fusion | bytes 8388736 | tf_op jit(solution)/shard_map/jit(_take)/gather | solution.py:208
  55.6 6.5 %copy.17 = bf16[32,128,512]{1,2,0:T(8,128)(2,1)} copy(bf16[32,128,512]{2,1,0:T(8,128)(2,1)} %gather_fusion.1) | data formatting | bytes 8388608 | tf_op jit(solution)/shard_map/jit(_take)/gather | solution.py:208
  62.1 7.0 %bitcast_subtract_fusion = f32[4,8,128,512]{2,3,1,0:T(8,128)} fusion(f32[4,8,128]{2,1,0:T(8,128)S(1)} %get-tuple-element.3, bf16[4,8,128,512]{2,3,1,0:T(8,128)(2,1)} %bitcast.53, pred[4,8]{1,0:T(4,128)(4,1)S(1)} %compare_and_fusion.2, bf16[4,128,512,1]{2,1,3,0:T(8,128)(2,1)S(1)} %bitcast.51, bf16[4,8,128,128]{3,2,1,0:T(8,128)(2,1)S(1)} %copy-done.3), kind=kOutput, calls=%fused_computation.13 | convolution fusion | flops 545259520 | bytes 14172192 | tf_op jit(solution)/shard_map/rtab,rad->rtbd/dot_general | solution.py:219
  69.1 10.3 %copy.27 = f32[4,8,128,512]{3,1,2,0:T(8,128)} copy(f32[4,8,128,512]{2,3,1,0:T(8,128)} %bitcast_subtract_fusion) | data formatting | bytes 16777216
  79.4 5.5 %fusion.29 = f32[12,65536]{1,0:T(8,128)S(1)} fusion(f32[32,65536]{1,0:T(8,128)} %bitcast.52, s32[32]{0:T(128)S(1)} %reshape.170), kind=kOutput, calls=%fused_computation.46 | convolution fusion | flops 301990272 | bytes 11534464 | tf_op jit(solution)/shard_map/tc,tf->cf/dot_general | solution.py:226
  84.9 0.0 copy-start.2
  84.9 2.0 %copy-done.2 = f32[12,65536]{1,0:T(8,128)} copy-done((f32[12,65536]{1,0:T(8,128)}, f32[12,65536]{1,0:T(8,128)S(1)}, u32[]{:S(2)}) %copy-start.2) | copy-done | bytes 3145752
  86.9 0.2 slice.18
  87.1 1.5 convert_element_type.40
  88.5 5.9 %all-to-all-start.1 = ((bf16[128,8,512]{2,1,0:T(8,128)(2,1)}), bf16[128,8,512]{2,1,0:T(8,128)(2,1)}, u32[]{:S(2)}, u32[]{:S(2)}) async-start(bf16[128,8,512]{2,1,0:T(8,128)(2,1)} %convert_element_type.40), calls=%async_computation.1 | async-start | bytes 2097152 | tf_op jit(solution)/shard_map/all_to_all | solution.py:236
  94.5 1.6 convolution_subtract_fusion
  96.1 2.7 %slice.15 = f32[4,65536]{1,0:T(4,128)} slice(f32[12,65536]{1,0:T(8,128)} %copy-done.2), slice={[0:4], [0:65536]} | slice | bytes 2097152 | tf_op jit(solution)/shard_map/slice | solution.py:232
  98.7 1.9 %reshape.173 = f32[512,512]{1,0:T(8,128)S(1)} reshape(f32[4,65536]{1,0:T(4,128)} %slice.15) | data formatting | bytes 2097152 | tf_op jit(solution)/shard_map/reshape | solution.py:232
  100.7 3.7 %fusion.7 = f32[4,512,128,1]{1,2,3,0:T(8,128)S(1)} fusion(bf16[4,8,128,128]{3,2,1,0:T(8,128)(2,1)S(1)} %copy-done.3, bf16[4,8,128,512]{2,3,1,0:T(8,128)(2,1)} %bitcast.54, pred[4,8]{1,0:T(4,128)(4,1)S(1)} %compare_and_fusion.2), kind=kOutput, calls=%fused_computation.17 | convolution fusion | flops 538968064 | bytes 6291488 | tf_op jit(solution)/shard_map/rtab,rtbd->rad/dot_general | solution.py:211
  104.4 0.2 fusion.20
  104.7 8.5 %all-to-all-done.1 = bf16[128,8,512]{2,1,0:T(8,128)(2,1)} async-done(((bf16[128,8,512]{2,1,0:T(8,128)(2,1)}), bf16[128,8,512]{2,1,0:T(8,128)(2,1)}, u32[]{:S(2)}, u32[]{:S(2)}) %all-to-all-start.1) | async-done | bytes 1048608 | tf_op jit(solution)/shard_map/all_to_all | solution.py:236
  113.1 1.9 %fusion.17 = f32[512,512]{1,0:T(8,128)S(1)} fusion(f32[512,512]{1,0:T(8,128)S(1)} %fusion.20, bf16[128,8,512]{2,1,0:T(8,128)(2,1)} %all-to-all-done.1, s32[1024]{0:T(1024)S(1)} %reshape_squeeze.9, pred[1024]{0:T(1024)(128)(4,1)S(1)} %lt.86, f32[512]{0:T(512)S(1)} %add_rsqrt_fusion), kind=kOutput, calls=%fused_computation.29 | convolution fusion | flops 538443776 | bytes 3152896 | tf_op jit(solution)/shard_map/dot_general | solution.py:242
  115.1 1.4 scatter_fusion
  116.5 17.2 %fusion.13 = bf16[512,1024]{1,0:T(8,128)(2,1)} fusion(bf16[1024,4096]{1,0:T(8,128)(2,1)} %param.11, f32[512,4096]{1,0:T(8,128)} %copy-done.9, bf16[4096,512]{1,0:T(8,128)(2,1)} %param.12, f32[512,512]{1,0:T(8,128)S(1)} %scatter_fusion), kind=kOutput, calls=%fused_computation.27 | convolution fusion | flops 6483083264 | bytes 23068672 | tf_op jit(solution)/shard_map/dot_general | solution.py:257
  133.7 7.4 %convolution_convert_fusion = bf16[4096,512]{1,0:T(8,128)(2,1)S(1)} fusion(f32[512,512]{1,0:T(8,128)S(1)} %scatter_fusion, f32[512,4096]{1,0:T(8,128)} %copy-done.9), kind=kOutput, calls=%fused_computation.15 | convolution fusion | flops 2168717312 | bytes 13631488 | tf_op jit(solution)/shard_map/dot_general | solution.py:261
  141.1 27.4 %scatter_sum.1 = f32[32,512]{1,0:T(8,128)S(1)} custom-call(bf16[64,2,32,512]{3,2,1,0:T(8,128)(2,1)S(1)} %bitcast.50), custom_call_target="tpu_custom_call" | custom-call | tf_op jit(solution)/shard_map/scatter_sum/pallas_call | solution.py:145
  168.5 0.6 copy.31
  (19 shorter events, 0.1 us)
Async XLA Ops:
  0.6 4.1 %copy-start = (bf16[512,1024]{1,0:T(8,128)(2,1)S(1)}, bf16[512,1024]{1,0:T(8,128)(2,1)}, u32[]{:S(2)}) copy-start(bf16[512,1024]{1,0:T(8,128)(2,1)} %param.10) | copy-start | bytes 3145732
  4.8 7.1 %copy-start.7 = (bf16[4096,512]{1,0:T(8,128)(2,1)S(1)}, bf16[4096,512]{1,0:T(8,128)(2,1)}, u32[]{:S(2)}) copy-start(bf16[4096,512]{1,0:T(8,128)(2,1)} %param.12) | copy-start | bytes 12582916
  11.8 3.2 %copy-start.9 = (f32[512,4096]{1,0:T(8,128)}, f32[512,4096]{1,0:T(8,128)S(1)}, u32[]{:S(2)}) copy-start(f32[512,4096]{1,0:T(8,128)S(1)} %fusion.39) | copy-start | bytes 25165828
  15.1 16.4 %copy-start.5 = (s32[4,8]{1,0:T(4,128)S(1)}, s32[4,8]{1,0:T(4,128)}, u32[]{:S(2)}) copy-start(s32[4,8]{1,0:T(4,128)} %param.14) | copy-start | bytes 388
  15.1 16.7 %copy-start.8 = (s32[64]{0:T(128)S(1)}, s32[64]{0:T(128)}, u32[]{:S(2)}) copy-start(s32[64]{0:T(128)} %param.18) | copy-start | bytes 772
  20.3 30.2 %all-to-all-start = ((bf16[128,8,512]{2,1,0:T(8,128)(2,1)}), bf16[128,8,512]{2,1,0:T(8,128)(2,1)S(1)}, u32[]{:S(2)}, u32[]{:S(2)}) async-start(bf16[128,8,512]{2,1,0:T(8,128)(2,1)} %fusion.22), calls=%async_computation | async-start | bytes 2097152 | tf_op jit(solution)/shard_map/all_to_all | solution.py:203
  50.5 1.0 copy-start.4
  55.6 6.5 %copy-start.3 = (bf16[4,8,128,128]{3,2,1,0:T(8,128)(2,1)S(1)}, bf16[4,8,128,128]{3,2,1,0:T(8,128)(2,1)}, u32[]{:S(2)}) copy-start(bf16[4,8,128,128]{3,2,1,0:T(8,128)(2,1)} %param.15) | copy-start | bytes 3145732
  79.4 15.1 %copy-start.6 = (s32[64]{0:T(128)S(1)}, s32[64]{0:T(128)}, u32[]{:S(2)}) copy-start(s32[64]{0:T(128)} %param.19) | copy-start | bytes 772
  84.9 2.0 %copy-start.2 = (f32[12,65536]{1,0:T(8,128)}, f32[12,65536]{1,0:T(8,128)S(1)}, u32[]{:S(2)}) copy-start(f32[12,65536]{1,0:T(8,128)S(1)} %fusion.29) | copy-start | bytes 9437188
  88.5 24.6 %all-to-all-start.1 = ((bf16[128,8,512]{2,1,0:T(8,128)(2,1)}), bf16[128,8,512]{2,1,0:T(8,128)(2,1)}, u32[]{:S(2)}, u32[]{:S(2)}) async-start(bf16[128,8,512]{2,1,0:T(8,128)(2,1)} %convert_element_type.40), calls=%async_computation.1 | async-start | bytes 2097152 | tf_op jit(solution)/shard_map/all_to_all | solution.py:236
  133.7 35.5 %copy-start.1 = (bf16[512,1024]{1,0:T(8,128)(2,1)S(1)}, bf16[512,1024]{1,0:T(8,128)(2,1)}, u32[]{:S(2)}) copy-start(bf16[512,1024]{1,0:T(8,128)(2,1)} %param.10) | copy-start | bytes 3145732

commit v2 on v1

--- a/solution.py
+++ b/solution.py
@@ -167,6 +167,148 @@
     )(partial)
 
 
+BLOCK = 128
+FIRST = (((0,), (0,)), ((), ()))
+
+
+def block_rows(index):
+    return pl.ds(pl.multiple_of(index * BLOCK, BLOCK), BLOCK)
+
+
+def pieces_of(sums):
+    high = sums.astype(jnp.bfloat16)
+    rest = sums - high.astype(jnp.float32)
+    middle = rest.astype(jnp.bfloat16)
+    low = (rest - middle.astype(jnp.float32)).astype(jnp.bfloat16)
+    lane = lax.broadcasted_iota(jnp.int32, sums.shape, 1)
+    wide = [piece.astype(jnp.float32) for piece in (high, middle, low)]
+    chosen = jnp.where(lane == 0, wide[0], jnp.where(lane == 1, wide[1], wide[2]))
+    return jnp.where(lane < 3, chosen, 0.0).astype(jnp.bfloat16)
+
+
+def outgoing_kernel(column_ref, projected_ref, weight_ref, sends_ref, unit_ref, rowsum_ref, out_ref, total):
+    width = projected_ref.shape[1]
+    ones = jnp.ones((BLOCK, BLOCK), jnp.bfloat16)
+    for block in range(4):
+        rows = slice(block * BLOCK, (block + 1) * BLOCK)
+        joined = weight_ref[block * 8].astype(jnp.float32)
+        for tile in range(1, 8):
+            joined = joined + weight_ref[block * 8 + tile].astype(jnp.float32)
+        rowsum = jnp.sum(joined, axis=1, keepdims=True)
+        rowsum_ref[rows] = jnp.broadcast_to(rowsum, (BLOCK, BLOCK))
+        unit_ref[rows] = (projected_ref[rows] * lax.rsqrt(1.0 + rowsum)).astype(jnp.bfloat16)
+    total[...] = jnp.zeros_like(total)
+    for block in range(4):
+        rows = slice(block * BLOCK, (block + 1) * BLOCK)
+        operand = jnp.concatenate([unit_ref[rows], ones], axis=1)
+        for tile in range(4, 8):
+            spot = column_ref[block, tile] - 4
+            total[spot] += lax.dot_general(
+                weight_ref[block * 8 + tile], operand, FIRST, preferred_element_type=jnp.float32
+            )
+    unit = unit_ref[...]
+    for block in range(8):
+        rows = slice(block * BLOCK, (block + 1) * BLOCK)
+        picks = (
+            sends_ref[rows] == lax.broadcasted_iota(jnp.int32, (BLOCK, unit.shape[0]), 1)
+        ).astype(jnp.bfloat16)
+        out_ref[rows, :width] = jnp.dot(picks, unit, preferred_element_type=jnp.float32).astype(
+            jnp.bfloat16
+        )
+        out_ref[rows, width : 2 * width] = total[block, :, :width].astype(jnp.bfloat16)
+        out_ref[rows, 2 * width :] = pieces_of(total[block, :, width:])
+
+
+def local_kernel(
+    column_ref, projected_ref, unit_ref, rowsum_ref, weight_ref, label_rows_ref, label_class_ref,
+    prototypes_ref, base_ref, total
+):
+    width = projected_ref.shape[1]
+    ones = jnp.ones((BLOCK, BLOCK), jnp.bfloat16)
+    total[...] = jnp.zeros_like(total)
+    classes = prototypes_ref.shape[0]
+    labels = label_rows_ref.shape[1]
+    table = (
+        label_class_ref[...] == lax.broadcasted_iota(jnp.int32, (labels, classes), 1)
+    ).astype(jnp.bfloat16)
+    targets = jnp.dot(table, prototypes_ref[...], preferred_element_type=jnp.float32).astype(
+        jnp.bfloat16
+    )
+    for block in range(4):
+        rows = slice(block * BLOCK, (block + 1) * BLOCK)
+        operand = jnp.concatenate([unit_ref[rows], ones], axis=1)
+        near = jnp.zeros((BLOCK, width), jnp.float32)
+        for tile in range(4):
+            spot = column_ref[block, tile]
+            weight = weight_ref[block * 8 + tile]
+            total[spot] += lax.dot_general(
+                weight, operand, FIRST, preferred_element_type=jnp.float32
+            )
+            near = near + jnp.dot(
+                weight, unit_ref[block_rows(spot)], preferred_element_type=jnp.float32
+            )
+        base_ref[rows] = near
+    for block in range(4):
+        rows = slice(block * BLOCK, (block + 1) * BLOCK)
+        rowsum = rowsum_ref[rows, :1]
+        unit = unit_ref[rows].astype(jnp.float32)
+        row_term = rowsum * unit - base_ref[rows]
+        own_term = total[block, :, width : width + 1] * unit - total[block, :, :width]
+        spots = label_rows_ref[...] == (
+            lax.broadcasted_iota(jnp.int32, (BLOCK, labels), 0) + block * BLOCK
+        )
+        marked = jnp.sum(spots.astype(jnp.float32), axis=1, keepdims=True)
+        wanted = jnp.dot(
+            spots.astype(jnp.bfloat16), targets, preferred_element_type=jnp.float32
+        )
+        base_ref[rows] = (row_term + own_term) * lax.rsqrt(1.0 + rowsum) + (
+            marked * projected_ref[rows] - wanted
+        )
+
+
+def merge_kernel(
+    column_ref, message_ref, unit_ref, rowsum_ref, base_ref, weight_ref, sends_ref, grad_ref
+):
+    width = unit_ref.shape[1]
+    slots = message_ref.shape[0]
+    for block in range(4):
+        rows = slice(block * BLOCK, (block + 1) * BLOCK)
+        picks = (
+            sends_ref[...]
+            == lax.broadcasted_iota(jnp.int32, (BLOCK, slots), 0) + block * BLOCK
+        ).astype(jnp.bfloat16)
+        back = jnp.dot(picks, message_ref[:, width:], preferred_element_type=jnp.float32)
+        sums = back[:, width : width + 1] + back[:, width + 1 : width + 2]
+        sums = sums + back[:, width + 2 : width + 3]
+        far = sums * unit_ref[rows].astype(jnp.float32) - back[:, :width]
+        for tile in range(4, 8):
+            spot = column_ref[block, tile] - 4
+            far = far - jnp.dot(
+                weight_ref[block * 8 + tile],
+                message_ref[block_rows(spot), :width],
+                preferred_element_type=jnp.float32,
+            )
+        grad_ref[rows] = (
+            base_ref[rows] + far * lax.rsqrt(1.0 + rowsum_ref[rows, :1])
+        ).astype(jnp.bfloat16)
+
+
+def on_core(kernel, name, count, outs, scratch=(), flops=0, moved_bytes=0):
+    return pl.pallas_call(
+        kernel,
+        out_shape=outs,
+        in_specs=[pl.BlockSpec(memory_space=pltpu.SMEM)]
+        + [pl.BlockSpec(memory_space=pltpu.VMEM)] * (count - 1),
+        out_specs=jax.tree.map(lambda _: pl.BlockSpec(memory_space=pltpu.VMEM), outs),
+        scratch_shapes=list(scratch),
+        cost_estimate=pl.CostEstimate(
+            flops=flops, bytes_accessed=moved_bytes, transcendentals=0
+        ),
+        compiler_params=pltpu.CompilerParams(vmem_limit_bytes=48 << 20),
+        name=name,
+    )
+
+
 def body(
     embeds,
     weight_in,
@@ -180,76 +322,63 @@
     label_class,
 ):
     node_count = embeds.shape[0]
-    block_count = tile_weight.shape[0]
-    tile_count = tile_weight.shape[1]
-    block_size = tile_weight.shape[2]
     width_out = weight_out.shape[1]
     dom_count = lax.axis_size("dom")
     rep_count = lax.axis_size("rep")
     peer_count = dom_count * rep_count
     slot_count = send_rows.shape[2]
+    slots = peer_count * slot_count
+    message = 2 * width_out + BLOCK
+    slot_mask = (
+        lax.broadcasted_iota(jnp.int32, (peer_count, slot_count), 1) < send_count[0][:, None]
+    )
+    sends = jnp.where(slot_mask, send_rows[0], -1)
     pre_act = jnp.dot(embeds, weight_in, preferred_element_type=jnp.float32)
     hidden = gelu_value(pre_act).astype(jnp.bfloat16)
     projected = jnp.dot(hidden, weight_out, preferred_element_type=jnp.float32)
-    rowsum = jnp.sum(tile_weight, axis=(1, 3), dtype=jnp.float32).reshape(node_count)
-    scaling = lax.rsqrt(1.0 + rowsum)
-    unit_rows = (projected * scaling[:, None]).astype(jnp.bfloat16)
-    slot_mask = (
-        lax.broadcasted_iota(jnp.int32, (peer_count, slot_count), 1) < send_count[0][:, None]
-    )
-    flat_sends = send_rows[0].reshape(peer_count * slot_count)
-    outgoing = jnp.take(unit_rows, flat_sends, axis=0).reshape(peer_count, slot_count, width_out)
-    outgoing = jnp.where(slot_mask[:, :, None], outgoing, jnp.zeros_like(outgoing))
-    incoming = lax.all_to_all(outgoing, ("dom", "rep"), split_axis=0, concat_axis=0, tiled=True)
-    incoming = incoming.reshape(peer_count * slot_count, width_out)
-    extended = jnp.concatenate([unit_rows, incoming], axis=0).reshape(-1, block_size, width_out)
-    total_blocks = extended.shape[0]
-    flat_columns = tile_column.reshape(block_count * tile_count)
-    sources = jnp.take(extended, flat_columns, axis=0).reshape(
-        block_count, tile_count, block_size, width_out
-    )
-    neighbour = jnp.einsum(
-        "rtab,rtbd->rad", tile_weight, sources, preferred_element_type=jnp.float32
-    )
-    row_term = rowsum[:, None] * unit_rows.astype(jnp.float32) - neighbour.reshape(
-        node_count, width_out
-    )
-    unit_blocks = unit_rows.reshape(block_count, block_size, width_out)
-    column_sum = jnp.sum(tile_weight, axis=2, dtype=jnp.float32)
-    column_term = column_sum[:, :, :, None] * sources.astype(jnp.float32) - jnp.einsum(
-        "rtab,rad->rtbd", tile_weight, unit_blocks, preferred_element_type=jnp.float32
-    )
-    selector = (
-        flat_columns[:, None]
-        == lax.broadcasted_iota(jnp.int32, (block_count * tile_count, total_blocks), 1)
-    ).astype(jnp.float32)
-    gathered_terms = jnp.einsum(
-        "tc,tf->cf",
-        selector,
-        column_term.reshape(block_count * tile_count, block_size * width_out),
-        precision=lax.Precision.HIGHEST,
-    )
-    own_term = gathered_terms[:block_count].reshape(node_count, width_out)
-    returned = (
-        gathered_terms[block_count:].reshape(peer_count, slot_count, width_out).astype(jnp.bfloat16)
-    )
-    arrived = lax.all_to_all(returned, ("dom", "rep"), split_axis=0, concat_axis=0, tiled=True)
-    back_rows = arrived.reshape(peer_count * slot_count, width_out)
-    placement = (
-        flat_sends[None, :]
-        == lax.broadcasted_iota(jnp.int32, (node_count, peer_count * slot_count), 0)
-    ) & slot_mask.reshape(peer_count * slot_count)[None, :]
-    back_sum = jnp.dot(
-        placement.astype(jnp.bfloat16), back_rows, preferred_element_type=jnp.float32
-    )
-    grad_proj = (row_term + own_term + back_sum) * scaling[:, None]
-    class_table = (
-        label_class[:, None]
-        == lax.broadcasted_iota(jnp.int32, (label_class.shape[0], prototypes.shape[0]), 1)
-    ).astype(jnp.bfloat16)
-    targets = jnp.dot(class_table, prototypes, preferred_element_type=jnp.float32)
-    grad_proj = grad_proj.at[label_rows].add(jnp.take(projected, label_rows, axis=0) - targets)
-    grad_node = grad_proj.astype(jnp.bfloat16)
+    weights = tile_weight.reshape(-1, BLOCK, BLOCK)
+    unit_rows, rowsum, outgoing = on_core(
+        outgoing_kernel,
+        "outgoing",
+        4,
+        (
+            jax.ShapeDtypeStruct((node_count, width_out), jnp.bfloat16),
+            jax.ShapeDtypeStruct((node_count, BLOCK), jnp.float32),
+            jax.ShapeDtypeStruct((slots, message), jnp.bfloat16),
+        ),
+        [pltpu.VMEM((8, BLOCK, width_out + BLOCK), jnp.float32)],
+    )(tile_column, projected, weights, sends.reshape(slots, 1))
+    arrived = lax.all_to_all(
+        outgoing.reshape(peer_count, slot_count, message),
+        ("dom", "rep"),
+        split_axis=0,
+        concat_axis=0,
+        tiled=True,
+    ).reshape(slots, message)
+    base = on_core(
+        local_kernel,
+        "local_terms",
+        8,
+        jax.ShapeDtypeStruct((node_count, width_out), jnp.float32),
+        [pltpu.VMEM((4, BLOCK, width_out + BLOCK), jnp.float32)],
+        flops=2 * 32 * 128 * 128 * 640,
+        moved_bytes=6 << 20,
+    )(
+        tile_column,
+        projected,
+        unit_rows,
+        rowsum,
+        weights,
+        label_rows.reshape(1, -1),
+        label_class.reshape(-1, 1),
+        prototypes,
+    )
+    grad_node = on_core(
+        merge_kernel,
+        "merge",
+        7,
+        jax.ShapeDtypeStruct((node_count, width_out), jnp.bfloat16),
+    )(tile_column, arrived, unit_rows, rowsum, base, weights, sends.reshape(1, slots))
     grad_hidden = lax.dot_general(
         grad_node, weight_out, (((1,), (1,)), ((), ())), preferred_element_type=jnp.float32
     )

time: 170 us -> 125 us (0.74)
  matrix products: 54.1 us -> 34.8 us
  local copies, waits for them, and re-layouts: 35.9 us -> 17.5 us
  Pallas kernels: 27.4 us -> 35.3 us
  other arithmetic: 7.27 us -> 0.89 us
  starting transfers between devices: 17.1 us -> 11.3 us
  waiting for transfers between devices: 26.4 us -> 23.3 us
    dot_general x5 -> x0, matrix products: 19.7 us -> none  [the longest x1 7.04 us: body(): jnp.einsum('rtab,rad->rtbd', tile_weight, unit_blocks, preferred_element_...]
    gather x4 -> x0, local copies, waits for them, and re-layouts: 13.9 us -> none  [the longest x2 9.25 us: body(): jnp.take(extended, flat_columns, axis=0)]
    pallas_call x0 -> x3, Pallas kernels: none -> 7.86 us  [the longest x1 2.78 us: body(): on_core(local_kernel, 'local_terms', 8, jax.ShapeDtypeStruct((node_count,...]
    all_to_all x2 -> x1, starting transfers between devices: 17.1 us -> 11.3 us  [body(): lax.all_to_all(outgoing.reshape(peer_count, slot_count, message), ('dom',...]
    all_to_all x2 -> x1, waiting for transfers between devices: 26.4 us -> 23.3 us  [body(): lax.all_to_all(outgoing.reshape(peer_count, slot_count, message), ('dom',...]
    slice x2 -> x0, local copies, waits for them, and re-layouts: 2.88 us -> none  [the longest x1 2.7 us: body(): own_term = gathered_terms[:block_count].reshape(node_count, width_out)]
    reshape x3 -> x1, local copies, waits for them, and re-layouts: 2.11 us -> 0.1 us  [body(): label_class.reshape(-1, 1)]
    unnamed x23 -> x46, local copies, waits for them, and re-layouts: 15.2 us -> 16.8 us
  transfers between devices with their start and end apart: 2 -> 1, of which waited for: 2 -> 1; matrix products, arithmetic and copies ran while one was open for 7% -> 0% of each run, Pallas kernels for 0% -> 2%
where the time goes in v2:
time: 125 us; the launch traced here: 124 us
  Pallas kernels  35.3 us (28%)
  matrix products  34.8 us (28%)
  waiting for transfers between devices  23.3 us (19%)
  local copies, waits for them, and re-layouts  17.5 us (14%)
  starting transfers between devices  11.3 us (9%)
    pallas_call x1, Pallas kernels, scatter_sum(): pl.pallas_call(functools.partial(scatter_sum_kernel, factor), out_shape=j...  27.4 us
    all_to_all x1, waiting for transfers between devices, body(): lax.all_to_all(outgoing.reshape(peer_count, slot_count, message), ('dom',...  23.3 us
    dot_general x1, matrix products, body(): lax.dot_general(grad_pre, weight_in, (((1,), (1,)), ((), ())), preferred_...  17.7 us
    unnamed x46, local copies, waits for them, and re-layouts  16.8 us
    all_to_all x1, starting transfers between devices, body(): lax.all_to_all(outgoing.reshape(peer_count, slot_count, message), ('dom',...  11.3 us
    dot_general x1, matrix products, body(): lax.dot_general(hidden, grad_node, (((0,), (0,)), ((), ())), preferred_el...  7.3 us
    dot_general x1, matrix products, body(): pre_act = jnp.dot(embeds, weight_in, preferred_element_type=jnp.float32)  7.05 us
    pallas_call x1, Pallas kernels, body(): on_core(local_kernel, 'local_terms', 8, jax.ShapeDtypeStruct((node_count,...  2.78 us
  transfers between devices with their start and end apart: 1, of which 1 were waited for; matrix products, arithmetic and copies ran while one was open for 0% of the time, Pallas kernels for 2%

profile of v2, /device:TPU:0, one launch (start us, length us, event | category | flops | bytes accessed | tf_op | source)
XLA Modules:
  0.0 123.9 jit_solution(7700825940249609948)
XLA Ops:
  0.6 0.0 copy-start
  0.6 0.8 iota_compare_fusion
  1.5 0.8 copy.15
  2.3 0.2 lt.35
  2.5 0.2 squeeze.7
  2.7 0.1 broadcast_select_fusion.sends_ref
  2.8 0.0 copy-done
  2.8 0.0 copy-start.20
  2.8 7.0 %fusion.15 = f32[512,4096]{1,0:T(8,128)S(1)} fusion(bf16[512,1024]{1,0:T(8,128)(2,1)S(1)} %copy-done, bf16[1024,4096]{1,0:T(8,128)(2,1)} %param.11), kind=kOutput, calls=%fused_computation.22 | convolution fusion | flops 4294967296 | bytes 17825792 | tf_op jit(solution)/shard_map/dot_general | solution.py:336
  9.8 0.0 copy-done.20
  9.8 0.0 copy-start.21
  9.9 0.0 copy-start.1
  9.9 0.0 copy-start.17
  9.9 0.0 copy-start.19
  9.9 0.0 copy-start.18
  9.9 2.7 %fusion.14.projected_ref = f32[512,512]{1,0:T(8,128)S(1)} fusion(bf16[4096,512]{1,0:T(8,128)(2,1)S(1)} %copy-done.20, f32[512,4096]{1,0:T(8,128)S(1)} %fusion.15), kind=kOutput, calls=%fused_computation.21 | convolution fusion | flops 2166358016 | bytes 13631488 | tf_op jit(solution)/shard_map/dot_general | solution.py:338
  12.6 0.5 copy-done.21
  13.1 0.0 copy-done.1
  13.1 0.0 copy-done.17
  13.1 2.6 %outgoing.1 = (bf16[512,512]{1,0:T(8,128)(2,1)S(1)}, f32[512,128]{1,0:T(8,128)S(1)}, bf16[1024,1152]{1,0:T(8,128)(2,1)S(1)}) custom-call(s32[4,8]{1,0:T(4,128)S(1)} %copy-done.17, f32[512,512]{1,0:T(8,128)S(1)} %fusion.14.projected_ref, bf16[32,128,128]{2,1,0:T(8,128)(2,1)S(1)} %bitcast.15, s32[1024,1]{1,0:T(8,128)S(1)} %broadcast_select_fusion.sends_ref), custom_call_target="tpu_custom_call" | custom-call | tf_op jit(solution)/shard_map/outgoing/pallas_call | solution.py:340
  15.7 0.0 copy-done.4
  15.7 1.5 %copy-done.8 = bf16[1024,1152]{1,0:T(8,128)(2,1)} copy-done((bf16[1024,1152]{1,0:T(8,128)(2,1)}, bf16[1024,1152]{1,0:T(8,128)(2,1)S(1)}, u32[]{:S(2)}) %copy-start.8) | copy-done | bytes 2359320
  17.2 0.8 copy-done.9
  18.0 0.7 copy-done.12
  18.7 11.3 %all-to-all-start = ((bf16[128,8,1152]{2,1,0:T(8,128)(2,1)}), bf16[128,8,1152]{2,1,0:T(8,128)(2,1)S(1)}, u32[]{:S(2)}, u32[]{:S(2)}) async-start(bf16[128,8,1152]{2,1,0:T(8,128)(2,1)} %bitcast.19), calls=%async_computation | async-start | bytes 4718592 | tf_op jit(solution)/shard_map/all_to_all | solution.py:351
  30.0 0.1 lt.34
  30.1 0.1 squeeze.6
  30.2 0.1 copy.18.label_class_ref
  30.3 1.2 copy-done.2
  31.5 1.2 copy-done.5
  32.8 1.0 copy-done.10
  33.8 0.9 copy-done.13
  34.7 1.2 copy-done.15
  36.0 2.8 %local_terms.1.base_ref = f32[512,512]{1,0:T(8,128)S(1)} custom-call(s32[4,8]{1,0:T(4,128)S(1)} %copy-done.17, f32[512,512]{1,0:T(8,128)S(1)} %copy-done.5, bf16[512,512]{1,0:T(8,128)(2,1)S(1)} %copy-done.10, f32[512,128]{1,0:T(8,128)S(1)} %copy-done.13, bf16[32,128,128]{2,1,0:T(8,128)(2,1)S(1)} %bitcast.16, s32[1,64]{1,0:T(1,128)S(1)} %bitcast.20, ...), custom_call_target="tpu_custom_call" | custom-call | flops 671088640 | bytes 6291456 | tf_op jit(solution)/shard_map/local_terms/pallas_call | solution.py:358
  38.7 0.0 copy-start.6
  38.8 1.0 copy-done.6
  39.7 23.3 %all-to-all-done = bf16[128,8,1152]{2,1,0:T(8,128)(2,1)S(1)} async-done(((bf16[128,8,1152]{2,1,0:T(8,128)(2,1)}), bf16[128,8,1152]{2,1,0:T(8,128)(2,1)S(1)}, u32[]{:S(2)}, u32[]{:S(2)}) %all-to-all-start) | async-done | bytes 2359328 | tf_op jit(solution)/shard_map/all_to_all | solution.py:351
  63.0 1.2 copy-done.3
  64.2 1.2 copy-done.7
  65.5 1.0 copy-done.11
  66.5 0.9 copy-done.14
  67.5 2.5 %merge.1 = bf16[512,512]{1,0:T(8,128)(2,1)S(1)} custom-call(s32[4,8]{1,0:T(4,128)S(1)} %copy-done.17, bf16[1024,1152]{1,0:T(8,128)(2,1)S(1)} %bitcast.14, bf16[512,512]{1,0:T(8,128)(2,1)S(1)} %copy-done.11, f32[512,128]{1,0:T(8,128)S(1)} %copy-done.14, f32[512,512]{1,0:T(8,128)S(1)} %copy-done.7, bf16[32,128,128]{2,1,0:T(8,128)(2,1)S(1)} %bitcast.17, ...), custom_call_target="tpu_custom_call" | custom-call | tf_op jit(solution)/shard_map/merge/pallas_call | solution.py:376
  70.0 0.0 copy-start.16
  70.0 0.9 copy-done.16
  70.8 17.7 %fusion.8 = bf16[512,1024]{1,0:T(8,128)(2,1)} fusion(bf16[1024,4096]{1,0:T(8,128)(2,1)} %param.11, f32[512,4096]{1,0:T(8,128)} %copy-done.21, bf16[512,512]{1,0:T(8,128)(2,1)} %copy-done.16, bf16[4096,512]{1,0:T(8,128)(2,1)} %param.12), kind=kOutput, calls=%fused_computation.12 | convolution fusion | flops 6482821120 | bytes 22544384 | tf_op jit(solution)/shard_map/dot_general | solution.py:386
  88.5 7.3 %convolution_convert_fusion = bf16[4096,512]{1,0:T(8,128)(2,1)S(1)} fusion(bf16[512,512]{1,0:T(8,128)(2,1)} %copy-done.16, f32[512,4096]{1,0:T(8,128)} %copy-done.21), kind=kOutput, calls=%fused_computation.10 | convolution fusion | flops 2168455168 | bytes 13107200 | tf_op jit(solution)/shard_map/dot_general | solution.py:390
  95.8 27.4 %scatter_sum.1 = f32[32,512]{1,0:T(8,128)S(1)} custom-call(bf16[64,2,32,512]{3,2,1,0:T(8,128)(2,1)S(1)} %bitcast.18), custom_call_target="tpu_custom_call" | custom-call | tf_op jit(solution)/shard_map/scatter_sum/pallas_call | solution.py:145
  123.3 0.6 copy.21
  (16 shorter events, 0.0 us)
Async XLA Ops:
  0.6 2.1 %copy-start = (bf16[512,1024]{1,0:T(8,128)(2,1)S(1)}, bf16[512,1024]{1,0:T(8,128)(2,1)}, u32[]{:S(2)}) copy-start(bf16[512,1024]{1,0:T(8,128)(2,1)} %param.10) | copy-start | bytes 3145732
  2.8 7.1 %copy-start.20 = (bf16[4096,512]{1,0:T(8,128)(2,1)S(1)}, bf16[4096,512]{1,0:T(8,128)(2,1)}, u32[]{:S(2)}) copy-start(bf16[4096,512]{1,0:T(8,128)(2,1)} %param.12) | copy-start | bytes 12582916
  9.8 3.2 %copy-start.21 = (f32[512,4096]{1,0:T(8,128)}, f32[512,4096]{1,0:T(8,128)S(1)}, u32[]{:S(2)}) copy-start(f32[512,4096]{1,0:T(8,128)S(1)} %fusion.15) | copy-start | bytes 25165828
  9.9 3.2 %copy-start.1 = (bf16[4,8,128,128]{3,2,1,0:T(8,128)(2,1)S(1)}, bf16[4,8,128,128]{3,2,1,0:T(8,128)(2,1)}, u32[]{:S(2)}) copy-start(bf16[4,8,128,128]{3,2,1,0:T(8,128)(2,1)} %param.15) | copy-start | bytes 3145732
  9.9 3.2 %copy-start.17 = (s32[4,8]{1,0:T(4,128)S(1)}, s32[4,8]{1,0:T(4,128)}, u32[]{:S(2)}) copy-start(s32[4,8]{1,0:T(4,128)} %column_ref.5) | copy-start | bytes 388
  9.9 20.3 %copy-start.19 = (s32[64]{0:T(128)S(1)}, s32[64]{0:T(128)}, u32[]{:S(2)}) copy-start(s32[64]{0:T(128)} %param.19) | copy-start | bytes 772
  9.9 20.4 %copy-start.18 = (s32[64]{0:T(128)S(1)}, s32[64]{0:T(128)}, u32[]{:S(2)}) copy-start(s32[64]{0:T(128)} %param.18) | copy-start | bytes 772
  13.1 2.6 %copy-start.4 = (f32[512,512]{1,0:T(8,128)}, f32[512,512]{1,0:T(8,128)S(1)}, u32[]{:S(2)}) copy-start(f32[512,512]{1,0:T(8,128)S(1)} %fusion.14.projected_ref) | copy-start | bytes 3145732
  15.7 1.5 %copy-start.8 = (bf16[1024,1152]{1,0:T(8,128)(2,1)}, bf16[1024,1152]{1,0:T(8,128)(2,1)S(1)}, u32[]{:S(2)}) copy-start(bf16[1024,1152]{1,0:T(8,128)(2,1)S(1)} %get-tuple-element.5) | copy-start | bytes 7077892
  17.2 0.8 copy-start.9
  18.0 0.7 copy-start.12
  18.7 44.4 %all-to-all-start = ((bf16[128,8,1152]{2,1,0:T(8,128)(2,1)}), bf16[128,8,1152]{2,1,0:T(8,128)(2,1)S(1)}, u32[]{:S(2)}, u32[]{:S(2)}) async-start(bf16[128,8,1152]{2,1,0:T(8,128)(2,1)} %bitcast.19), calls=%async_computation | async-start | bytes 4718592 | tf_op jit(solution)/shard_map/all_to_all | solution.py:351
  30.3 1.2 copy-start.2
  31.5 1.2 copy-start.5
  32.8 1.0 copy-start.10
  33.8 0.9 copy-start.13
  34.7 1.2 copy-start.15
  38.7 1.0 copy-start.6
  63.0 1.2 copy-start.3
  64.2 1.2 copy-start.7
  65.5 1.0 copy-start.11
  66.5 0.9 copy-start.14
  70.0 0.9 copy-start.16
